TPU v7x, 256 devices: a whole 4x4x8 slice. The times are simulated.
256 devices in a mesh: fsdp: 32 (over y, x, core), tp: 8 (over z).
Axes of the slice: x: 4, y: 4, z: 8, core: 2. Of those that a mesh axis runs over, the one named last changes fastest.
Arguments:
- dec_queries: bfloat16 [2, 64, 8192], P(None, 'fsdp', 'tp'), may hold values from -160 to 160
- cache_keys: bfloat16 [64, 4096, 1024], P('fsdp', None, 'tp'), may hold values from -5.2 to 5.2
- cached_value_rows: bfloat16 [64, 4096, 1024], P('fsdp', None, 'tp'), may hold values from -6 to 6
- step_keys: bfloat16 [2, 64, 1024], P(None, 'fsdp', 'tp'), may hold values from -6 to 6
- step_values: bfloat16 [2, 64, 1024], P(None, 'fsdp', 'tp'), may hold values from -6 to 6
- prompt_lengths: int32 [64], P('fsdp'), may hold values from 2 to 4096
- resp_embed: bfloat16 [512, 32, 8192], P('fsdp', None, 'tp'), may hold values from -520 to 520
- resp_ids: int32 [512, 32], P('fsdp'), may hold values from 0 to 152063
- resp_lengths: int32 [512], P('fsdp'), may hold values from 25 to 32
- dest_shard: int32 [512], P('fsdp'), may hold values from 0 to 31, as said below
- dest_offset: int32 [512], P('fsdp'), may hold values from 0 to 511, as said below
- norm_gain: float32 [8192], replicated, may hold values from 0.7 to 7
- w_q: bfloat16 [8192, 8192], P('fsdp', 'tp'), may hold values from -0.0625 to 0.0625
- key_value_weight: bfloat16 [8192, 2, 1024], P('fsdp', None, 'tp'), may hold values from -0.0625 to 0.0625
- bias_q: float32 [8192], P('tp'), may hold values from -3 to 3
- key_value_bias: float32 [2, 1024], P(None, 'tp'), may hold values from -3 to 3
Outputs:
- decode_out: bfloat16 [2, 64, 8192], P(None, 'fsdp', 'tp')
- packed_ids: int32 [16384], P('fsdp')
- ref_attn: bfloat16 [16384, 8192], P('fsdp', 'tp')
Inputs may be any that keep to these rules, and one draw needn't show every extreme that they name: `dest_shard`: each shard receives exactly 16 responses; the 16 responses held by one index of fsdp go 1 each to half of the shards and none to the others. The responses of one shard occupy disjoint runs from dest_offset to dest_offset + resp_lengths - 1 within its 512 positions.
All inputs are finite; a program needn't handle non-finite values.
Results may differ from a plain program's by a relative error of at most 0.005.
The roundings to bfloat16 on the way count: a program that leaves them out, or rounds other values in their place, can miss the bound.
Values may be sent and summed in bfloat16 or wider, within the bound.
No kernel may reach another device: no remote copies, remote signals or barrier semaphores. Data moves between devices by JAX's collectives and lax.ppermute only.
A program may use at most 128 MiB of HBM per device.

v0:
```python
import jax
import jax.numpy as jnp
from jax import lax
from jax.sharding import PartitionSpec as P

QUERY_HEADS = 64
KEY_VALUE_HEADS = 8
HEAD_SIZE = 128
rope_base = 1000000.0
eps_norm = 1e-06


def sent_together(arrays, axis, dim, along):
    ends, at = ([], 0)
    for a in arrays[:-1]:
        at += a.shape[along]
        ends.append(at)
    both = jnp.concatenate(arrays, axis=along)
    return tuple(jnp.split(lax.all_gather(both, axis, axis=dim, tiled=True), ends, axis=along))


def rotate_half(values, positions):
    half_dim = HEAD_SIZE // 2
    frequency = rope_base ** (-jnp.arange(half_dim, dtype=jnp.float32) * 2.0 / HEAD_SIZE)
    angles = positions.astype(jnp.float32)[:, None] * frequency[None, :]
    cosine = jnp.cos(angles)[:, None, :]
    sine_part = jnp.sin(angles)[:, None, :]
    lower_half = values[..., :half_dim]
    upper_half = values[..., half_dim:]
    return jnp.concatenate(
        [
            lower_half * cosine - upper_half * sine_part,
            upper_half * cosine + lower_half * sine_part,
        ],
        axis=-1,
    )


def decode_local(
    dec_queries, cache_keys, cached_value_rows, step_keys, step_values, prompt_lengths
):
    step_count, row_count, head_width = dec_queries.shape
    head_groups = QUERY_HEADS // KEY_VALUE_HEADS
    kv_local = cache_keys.shape[2] // HEAD_SIZE
    length = cache_keys.shape[1]
    score_scale = HEAD_SIZE ** (-0.5)
    query_rows = dec_queries.reshape(step_count, row_count, kv_local, head_groups, HEAD_SIZE)
    key_matrix = cache_keys.reshape(row_count, length, kv_local, HEAD_SIZE)
    value_matrix = cached_value_rows.reshape(row_count, length, kv_local, HEAD_SIZE)
    latest_key = step_keys.reshape(step_count, row_count, kv_local, HEAD_SIZE)
    latest_value = step_values.reshape(step_count, row_count, kv_local, HEAD_SIZE)
    cached = (
        jnp.einsum("srkgd,rckd->srkgc", query_rows, key_matrix, preferred_element_type=jnp.float32)
        * score_scale
    )
    live_mask = jnp.arange(length, dtype=jnp.int32)[None, :] < prompt_lengths[:, None]
    cached = jnp.where(live_mask[None, :, None, None, :], cached, -jnp.inf)
    recent = (
        jnp.einsum("srkgd,urkd->srkgu", query_rows, latest_key, preferred_element_type=jnp.float32)
        * score_scale
    )
    causal = jnp.arange(step_count)[None, :] <= jnp.arange(step_count)[:, None]
    recent = jnp.where(causal[:, None, None, None, :], recent, -jnp.inf)
    highest = jnp.maximum(jnp.max(cached, axis=-1), jnp.max(recent, axis=-1))[..., None]
    cached_w = jnp.exp(cached - highest)
    recent_w = jnp.exp(recent - highest)
    totals = jnp.sum(cached_w, axis=-1, keepdims=True) + jnp.sum(recent_w, axis=-1, keepdims=True)
    cached_w = (cached_w / totals).astype(jnp.bfloat16)
    recent_w = (recent_w / totals).astype(jnp.bfloat16)
    output = jnp.einsum(
        "srkgc,rckd->srkgd", cached_w, value_matrix, preferred_element_type=jnp.float32
    )
    output = output + jnp.einsum(
        "srkgu,urkd->srkgd", recent_w, latest_value, preferred_element_type=jnp.float32
    )
    return output.reshape(step_count, row_count, head_width).astype(jnp.bfloat16)


def attend_packed(query_raw, unscaled_pairs, doc_ids, token_row, covered):
    token_count = query_raw.shape[0]
    kv_count = unscaled_pairs.shape[2] // HEAD_SIZE
    head_groups = QUERY_HEADS // KEY_VALUE_HEADS
    query_rows = rotate_half(
        query_raw.reshape(token_count, kv_count * head_groups, HEAD_SIZE), token_row
    ).astype(jnp.bfloat16)
    key_matrix = rotate_half(
        unscaled_pairs[:, 0].reshape(token_count, kv_count, HEAD_SIZE), token_row
    ).astype(jnp.bfloat16)
    value_matrix = (
        unscaled_pairs[:, 1].reshape(token_count, kv_count, HEAD_SIZE).astype(jnp.bfloat16)
    )
    query_rows = query_rows.reshape(token_count, kv_count, head_groups, HEAD_SIZE)
    scores = jnp.einsum(
        "tkgd,skd->kgts", query_rows, key_matrix, preferred_element_type=jnp.float32
    ) * HEAD_SIZE ** (-0.5)
    indices = jnp.arange(token_count, dtype=jnp.int32)
    allowed = (doc_ids[:, None] == doc_ids[None, :]) & (indices[None, :] <= indices[:, None])
    scores = jnp.where(allowed, scores, -jnp.inf)
    highest = jnp.max(scores, axis=-1, keepdims=True)
    weights = jnp.exp(scores - highest)
    weights = (weights / jnp.sum(weights, axis=-1, keepdims=True)).astype(jnp.bfloat16)
    output = jnp.einsum("kgts,skd->tkgd", weights, value_matrix, preferred_element_type=jnp.float32)
    output = jnp.where(covered[:, None, None, None], output, 0.0)
    return output.reshape(token_count, kv_count * head_groups * HEAD_SIZE).astype(jnp.bfloat16)


def normalize(rows, norm_gain):
    wide = rows.astype(jnp.float32)
    return (
        wide
        * lax.rsqrt(jnp.mean(wide * wide, axis=1, keepdims=True) + eps_norm)
        * norm_gain[None, :]
    ).astype(jnp.bfloat16)


def on_device(
    dec_queries,
    cache_keys,
    cached_value_rows,
    step_keys,
    step_values,
    prompt_lengths,
    resp_embed,
    resp_ids,
    resp_lengths,
    dest_shard,
    dest_offset,
    norm_gain,
    w_q,
    key_value_weight,
    bias_q,
    key_value_bias,
):
    decode_out = decode_local(
        dec_queries, cache_keys, cached_value_rows, step_keys, step_values, prompt_lengths
    )
    nshard = lax.axis_size("fsdp")
    resp_count = resp_lengths.shape[0]
    resp_span = resp_embed.shape[1]
    packed_len = resp_count * resp_span
    capacity = 2 * resp_count // nshard
    indices = jnp.arange(resp_count, dtype=jnp.int32)
    earlier = (dest_shard[None, :] == dest_shard[:, None]) & (indices[None, :] < indices[:, None])
    pair_rank = jnp.sum(earlier.astype(jnp.int32), axis=1)
    placing = (dest_shard[:, None, None] == jnp.arange(nshard, dtype=jnp.int32)[None, :, None]) & (
        pair_rank[:, None, None] == jnp.arange(capacity, dtype=jnp.int32)[None, None, :]
    )
    slot_rows = jnp.einsum(
        "kpc,krx->pcrx",
        placing.astype(jnp.bfloat16),
        resp_embed,
        preferred_element_type=jnp.float32,
    ).astype(jnp.bfloat16)
    slot_ids = jnp.sum(jnp.where(placing[:, :, :, None], resp_ids[:, None, None, :], 0), axis=0)
    slot_lengths = jnp.sum(jnp.where(placing, resp_lengths[:, None, None], 0), axis=0)
    slot_offsets = jnp.sum(jnp.where(placing, dest_offset[:, None, None], 0), axis=0)
    slot_meta = jnp.stack([slot_lengths, slot_offsets], axis=-1)
    arrived, arrived_ids, arrived_meta = (
        lax.all_to_all(slot_rows, "fsdp", split_axis=0, concat_axis=0, tiled=True),
        lax.all_to_all(slot_ids, "fsdp", split_axis=0, concat_axis=0, tiled=True),
        lax.all_to_all(slot_meta, "fsdp", split_axis=0, concat_axis=0, tiled=True),
    )
    slot_total = nshard * capacity
    flat_rows = arrived.reshape(slot_total * resp_span, arrived.shape[3])
    flat_ids = arrived_ids.reshape(slot_total * resp_span)
    lengths_in = arrived_meta[:, :, 0].reshape(slot_total)
    offsets_in = arrived_meta[:, :, 1].reshape(slot_total)
    position = jnp.arange(packed_len, dtype=jnp.int32)
    inside = (position[:, None] >= offsets_in[None, :]) & (
        position[:, None] < (offsets_in + lengths_in)[None, :]
    )
    covered = jnp.any(inside, axis=1)
    slot_pick = jnp.sum(
        jnp.where(inside, jnp.arange(slot_total, dtype=jnp.int32)[None, :], 0), axis=1
    )
    token_row = jnp.where(
        covered, position - jnp.sum(jnp.where(inside, offsets_in[None, :], 0), axis=1), 0
    )
    source_row = jnp.where(covered, slot_pick * resp_span + token_row, 0)
    tokens = jnp.where(covered[:, None], flat_rows[source_row], jnp.zeros((), jnp.bfloat16))
    packed_ids = jnp.where(covered, flat_ids[source_row], -1).astype(jnp.int32)
    doc_ids = jnp.where(covered, slot_pick, -1)
    full_rows = lax.all_gather(tokens, "tp", axis=1, tiled=True)
    scaled_input = normalize(full_rows, norm_gain)
    q_width = w_q.shape[1]
    pair_width = key_value_weight.shape[1] * key_value_weight.shape[2]
    w_pairs = key_value_weight.reshape(key_value_weight.shape[0], pair_width)

    def add_rows(totals, piece_rows, start_row):
        columns = lax.dynamic_slice_in_dim(scaled_input, start_row, piece_rows.shape[0], 1)
        return totals + jnp.dot(columns, piece_rows, preferred_element_type=jnp.float32)

    empty_q = jnp.zeros((packed_len, q_width), jnp.float32)
    empty_pairs = jnp.zeros((packed_len, pair_width), jnp.float32)
    totals = (empty_q, empty_pairs)
    piece_rows = sent_together((w_q, w_pairs), "fsdp", 0, 1)
    start_row = jnp.int32(0)
    query_raw = add_rows(totals[0], piece_rows[0], start_row)
    unscaled_pairs = add_rows(totals[1], piece_rows[1], start_row)
    query_raw = query_raw + bias_q[None, :]
    unscaled_pairs = unscaled_pairs.reshape(packed_len, 2, pair_width // 2) + key_value_bias[None]
    ref_attn = attend_packed(query_raw, unscaled_pairs, doc_ids, token_row, covered)
    return (decode_out, packed_ids, ref_attn)


def solution(mesh):
    in_specs = (
        P(None, "fsdp", "tp"),
        P("fsdp", None, "tp"),
        P("fsdp", None, "tp"),
        P(None, "fsdp", "tp"),
        P(None, "fsdp", "tp"),
        P("fsdp"),
        P("fsdp", None, "tp"),
        P("fsdp", None),
        P("fsdp"),
        P("fsdp"),
        P("fsdp"),
        P(),
        P("fsdp", "tp"),
        P("fsdp", None, "tp"),
        P("tp"),
        P(None, "tp"),
    )
    out_specs = (P(None, "fsdp", "tp"), P("fsdp"), P("fsdp", "tp"))
    return jax.shard_map(
        on_device, mesh=mesh, in_specs=in_specs, out_specs=out_specs, check_vma=False
    )
```

profile of v0, /device:TPU:1, one launch (start us, length us, event | category | flops | bytes accessed | tf_op | source)
XLA Modules:
  0.0 290.8 jit_solution(11311541848920163075)
XLA Ops:
  7.2 0.0 copy-start
  7.2 1.0 convert_reduce_fusion
  8.2 0.8 select_reduce_fusion.4
  9.0 0.7 copy.91
  9.7 8.6 %all-to-all-start = ((s32[32,1,2]{2,1,0:T(1,128)}), s32[32,1,2]{2,1,0:T(1,128)S(1)}, u32[]{:S(2)}, u32[]{:S(2)}) async-start(s32[32,1,2]{2,1,0:T(1,128)} %copy.91), calls=%async_computation | async-start | bytes 32768 | tf_op jit(solution)/shard_map/all_to_all | solution.py:161
  18.3 2.2 convert_bitcast_fusion
  20.5 2.4 copy.94
  22.9 2.2 all-to-all-done
  25.2 5.3 %all-to-all-start.2 = ((bf16[32,1,32,1024]{3,2,1,0:T(8,128)(2,1)}), bf16[32,1,32,1024]{3,2,1,0:T(8,128)(2,1)}, u32[]{:S(2)}, u32[]{:S(2)}) async-start(bf16[32,1,32,1024]{3,2,1,0:T(8,128)(2,1)} %copy.94), calls=%async_computation.2 | async-start | bytes 4194304 | tf_op jit(solution)/shard_map/all_to_all | solution.py:159
  30.5 0.0 copy-start.5
  30.5 0.0 copy-start.3
  30.5 0.0 copy-start.4
  30.5 0.0 copy-start.11
  30.5 0.0 copy-start.8
  30.6 0.0 all-gather.3.cloned.1.call-start
  30.6 1.3 slice_reduce_fusion
  31.9 0.1 fusion.60
  32.0 0.1 select_reduce_fusion.1
  32.1 27.1 %all-to-all-done.2 = bf16[32,1,32,1024]{3,2,1,0:T(8,128)(2,1)} async-done(((bf16[32,1,32,1024]{3,2,1,0:T(8,128)(2,1)}), bf16[32,1,32,1024]{3,2,1,0:T(8,128)(2,1)}, u32[]{:S(2)}, u32[]{:S(2)}) %all-to-all-start.2) | async-done | bytes 2097184 | tf_op jit(solution)/shard_map/all_to_all | solution.py:159
  59.2 4.6 %gather_fusion.1 = bf16[512,1024]{1,0:T(8,128)(2,1)S(1)} fusion(bf16[1024,1024]{1,0:T(8,128)(2,1)} %bitcast.24, s32[1024]{0:T(1024)S(1)} %pad_clamp_fusion), kind=kCustom, calls=%fused_computation.1 | custom fusion | bytes 2099200 | tf_op jit(solution)/shard_map/gather | solution.py:180
  63.8 1.1 broadcast_select_fusion
  65.0 0.0 all-gather.3.cloned.1.call-update
  65.0 0.0 all-gather.5.cloned.1.call-start
  65.1 2.0 pad_maximum_fusion
  67.0 0.0 all-gather.5.cloned.1.call-update
  67.1 0.1 fusion.63
  67.1 0.7 select_reduce_fusion
  67.9 5.1 %all-to-all-start.1 = ((s32[32,1,32]{2,1,0:T(1,128)}), s32[32,1,32]{2,1,0:T(1,128)S(1)}, u32[]{:S(2)}, u32[]{:S(2)}) async-start(s32[32,1,32]{2,1,0:T(1,128)} %bitcast.18), calls=%async_computation.1 | async-start | bytes 32768 | tf_op jit(solution)/shard_map/all_to_all | solution.py:160
  73.0 0.1 convolution_multiply_fusion.1
  73.1 0.1 fusion.77
  73.2 0.1 iota_compare_fusion.3
  73.3 0.0 copy-start.9
  73.4 0.0 copy-start.10
  73.4 0.7 fusion.80
  74.1 0.1 fusion.67
  74.2 0.2 fusion.42
  74.5 0.1 fusion.71
  74.6 0.2 fusion.69
  74.8 2.1 fusion.33
  76.8 0.6 copy.100
  77.5 1.0 multiply_cosine_fusion
  78.4 0.2 fusion.41
  78.7 1.4 all-to-all-done.1
  80.0 0.5 broadcast.446
  80.5 0.7 reduce.16
  81.2 0.1 reshape.594
  81.3 2.3 gather_fusion
  83.6 0.6 broadcast_select_fusion.2
  84.2 75.0 %all-gather.3.cloned.1.call-done = bf16[512,8192]{1,0:T(8,128)(2,1)} async-done(((bf16[512,1024]{1,0:T(8,128)(2,1)}), bf16[512,8192]{1,0:T(8,128)(2,1)}) %all-gather.3.cloned.1.call-update) | async-done | bytes 8388624 | tf_op jit(solution)/shard_map/all_gather | solution.py:183
  159.2 5.1 %fusion = f32[512]{0:T(512)S(1)} fusion(bf16[512,8192]{1,0:T(8,128)(2,1)} %all-gather.3.cloned.1.call-done), kind=kLoop, calls=%fused_computation.4 | loop fusion | flops 12582400 | bytes 8390656 | tf_op jit(solution)/shard_map/reduce_sum | solution.py:111
  164.3 83.7 %all-gather.5.cloned.1.call-done = bf16[8192,1280]{1,0:T(8,128)(2,1)} async-done(((bf16[256,1280]{1,0:T(8,128)(2,1)}), bf16[8192,1280]{1,0:T(8,128)(2,1)}) %all-gather.5.cloned.1.call-update) | async-done | bytes 20971536 | tf_op jit(solution)/shard_map/all_gather | solution.py:19
  248.0 15.0 %add_bitcast_fusion = f32[64,8,8,128]{3,1,2,0:T(8,128)S(1)} fusion(bf16[8192,1280]{1,0:T(8,128)(2,1)} %all-gather.5.cloned.1.call-done, bf16[512,8192]{1,0:T(8,128)(2,1)} %all-gather.3.cloned.1.call-done, f32[8192]{0:T(1024)S(1)} %copy-done.9, f32[512]{0:T(512)S(1)} %add_rsqrt_fusion, f32[1024]{0:T(1024)S(1)} %copy-done.10), kind=kOutput, calls=%fused_computation.30 | convolution fusion | flops 8607236096 | bytes 27301888 | tf_op jit(solution)/shard_map/dot_general | solution.py:191
  263.0 0.5 copy.118
  263.5 0.0 copy-start.6
  263.5 8.2 %fusion.10 = f32[512,256]{0,1:T(8,128)} fusion(bf16[8192,1280]{1,0:T(8,128)(2,1)} %all-gather.5.cloned.1.call-done, bf16[512,8192]{1,0:T(8,128)(2,1)} %all-gather.3.cloned.1.call-done, f32[8192]{0:T(1024)S(1)} %copy-done.9, f32[512]{0:T(512)S(1)} %add_rsqrt_fusion), kind=kOutput, calls=%fused_computation.18 | convolution fusion | flops 2164260864 | bytes 13142016 | tf_op jit(solution)/shard_map/dot_general | solution.py:191
  271.8 1.2 copy.95
  273.1 1.4 fusion.58
  274.5 0.7 fusion.79
  275.2 0.8 subtract_convert_fusion
  276.0 2.2 fusion.6
  278.2 1.7 fusion.5
  279.9 0.0 copy-start.1
  280.0 2.7 fusion.20
  282.6 1.3 copy.101
  (29 shorter events, 0.2 us)
Async XLA Ops:
  7.2 66.2 %copy-start = (bf16[2,4096,128]{2,1,0:T(8,128)(2,1)S(1)}, bf16[2,4096,128]{2,1,0:T(8,128)(2,1)}, u32[]{:S(2)}) copy-start(bf16[2,4096,128]{2,1,0:T(8,128)(2,1)} %param.17) | copy-start | bytes 6291460
  9.7 15.5 %all-to-all-start = ((s32[32,1,2]{2,1,0:T(1,128)}), s32[32,1,2]{2,1,0:T(1,128)S(1)}, u32[]{:S(2)}, u32[]{:S(2)}) async-start(s32[32,1,2]{2,1,0:T(1,128)} %copy.91), calls=%async_computation | async-start | bytes 32768 | tf_op jit(solution)/shard_map/all_to_all | solution.py:161
  22.9 42.1 %copy-start.2 = (bf16[256,2,128]{2,1,0:T(2,128)(2,1)S(1)}, bf16[256,2,128]{2,1,0:T(2,128)(2,1)}, u32[]{:S(2)}) copy-start(bf16[256,2,128]{2,1,0:T(2,128)(2,1)} %param.29) | copy-start | bytes 393220
  25.2 34.1 %all-to-all-start.2 = ((bf16[32,1,32,1024]{3,2,1,0:T(8,128)(2,1)}), bf16[32,1,32,1024]{3,2,1,0:T(8,128)(2,1)}, u32[]{:S(2)}, u32[]{:S(2)}) async-start(bf16[32,1,32,1024]{3,2,1,0:T(8,128)(2,1)} %copy.94), calls=%async_computation.2 | async-start | bytes 4194304 | tf_op jit(solution)/shard_map/all_to_all | solution.py:159
  30.5 36.5 %copy-start.5 = (s32[16]{0:T(128)S(1)}, s32[16]{0:T(128)}, u32[]{:S(2)}) copy-start(s32[16]{0:T(128)} %param.25) | copy-start | bytes 196
  30.5 36.6 %copy-start.3 = (s32[16,32]{1,0:T(8,128)S(1)}, s32[16,32]{1,0:T(8,128)}, u32[]{:S(2)}) copy-start(s32[16,32]{1,0:T(8,128)} %param.23) | copy-start | bytes 6148
  30.5 42.4 %copy-start.4 = (bf16[2,2,1024]{2,1,0:T(2,128)(2,1)S(1)}, bf16[2,2,1024]{2,1,0:T(2,128)(2,1)}, u32[]{:S(2)}) copy-start(bf16[2,2,1024]{2,1,0:T(2,128)(2,1)} %param.16) | copy-start | bytes 24580
  30.5 42.5 %copy-start.11 = (bf16[2,2,128]{2,1,0:T(2,128)(2,1)S(1)}, bf16[2,2,128]{2,1,0:T(2,128)(2,1)}, u32[]{:S(2)}) copy-start(bf16[2,2,128]{2,1,0:T(2,128)(2,1)} %param.19) | copy-start | bytes 3076
  30.5 42.7 %copy-start.8 = (s32[2]{0:T(128)S(1)}, s32[2]{0:T(128)}, u32[]{:S(2)}) copy-start(s32[2]{0:T(128)} %param.21) | copy-start | bytes 28
  30.6 128.6 %all-gather.3.cloned.1.call-start = ((), (), s32[]{:S(2)}) async-start(), calls=%async_computation.3 | async-start | bytes 9437184 | tf_op jit(solution)/shard_map/all_gather | solution.py:183
  59.2 15.3 %copy-start.7 = (bf16[2,2,128]{2,1,0:T(2,128)(2,1)S(1)}, bf16[2,2,128]{2,1,0:T(2,128)(2,1)}, u32[]{:S(2)}) copy-start(bf16[2,2,128]{2,1,0:T(2,128)(2,1)} %param.20) | copy-start | bytes 3076
  65.0 183.0 %all-gather.5.cloned.1.call-start = ((), (), s32[]{:S(2)}) async-start(), calls=%async_computation.4 | async-start | bytes 21626880 | tf_op jit(solution)/shard_map/all_gather | solution.py:19
  67.9 12.2 %all-to-all-start.1 = ((s32[32,1,32]{2,1,0:T(1,128)}), s32[32,1,32]{2,1,0:T(1,128)S(1)}, u32[]{:S(2)}, u32[]{:S(2)}) async-start(s32[32,1,32]{2,1,0:T(1,128)} %bitcast.18), calls=%async_computation.1 | async-start | bytes 32768 | tf_op jit(solution)/shard_map/all_to_all | solution.py:160
  73.3 174.7 %copy-start.9 = (f32[8192]{0:T(1024)S(1)}, f32[8192]{0:T(1024)}, u32[]{:S(2)}) copy-start(f32[8192]{0:T(1024)} %param.27) | copy-start | bytes 98308
  73.4 174.7 %copy-start.10 = (f32[1024]{0:T(1024)S(1)}, f32[1024]{0:T(1024)}, u32[]{:S(2)}) copy-start(f32[1024]{0:T(1024)} %param.30) | copy-start | bytes 12292
  263.5 9.5 %copy-start.6 = (f32[2,128]{1,0:T(2,128)S(1)}, f32[2,128]{1,0:T(2,128)}, u32[]{:S(2)}) copy-start(f32[2,128]{1,0:T(2,128)} %param.31) | copy-start | bytes 3076
  279.9 4.0 %copy-start.1 = (bf16[2,4096,128]{2,1,0:T(8,128)(2,1)S(1)}, bf16[2,4096,128]{2,1,0:T(8,128)(2,1)}, u32[]{:S(2)}) copy-start(bf16[2,4096,128]{2,1,0:T(8,128)(2,1)} %param.17) | copy-start | bytes 6291460
Sparse Core Ops, SparseCore 0:
  65.1 94.0 all-gather.2
  161.7 86.2 all-gather.4
where the time goes:
time: 291 us
  waiting for transfers between devices  189 us (65%)
  matrix products  33.4 us (11%)
  starting transfers between devices  19.1 us (7%)
  other arithmetic  18.1 us (6%)
  local copies, waits for them, and re-layouts  16.3 us (6%)
  between operations  14.4 us (5%)
    all_gather x1, waiting for transfers between devices, sent_together(): lax.all_gather(both, axis, axis=dim, tiled=True)  83.7 us
    all_gather x1, waiting for transfers between devices, on_device(): full_rows = lax.all_gather(tokens, 'tp', axis=1, tiled=True)  75 us
    all_to_all x1, waiting for transfers between devices, on_device(): lax.all_to_all(slot_rows, 'fsdp', split_axis=0, concat_axis=0, tiled=True)  27.1 us
    dot_general x2, matrix products, add_rows(): jnp.dot(columns, piece_rows, preferred_element_type=jnp.float32)  23.3 us
    all_to_all x1, starting transfers between devices, on_device(): lax.all_to_all(slot_meta, 'fsdp', split_axis=0, concat_axis=0, tiled=True)  8.58 us
  transfers between devices with their start and end apart: 5, of which 5 were waited for; matrix products, arithmetic and copies ran while one was open for 8% of the time, Pallas kernels for 0%

commit v1 on v0

--- a/solution.py
+++ b/solution.py
@@ -8,6 +8,13 @@
 HEAD_SIZE = 128
 rope_base = 1000000.0
 eps_norm = 1e-06
+
+
+def all_by_exchange(array, mesh_axis, along):
+    size = lax.axis_size(mesh_axis)
+    blocks = jnp.stack([array for _ in range(size)])
+    blocks = lax.all_to_all(blocks, mesh_axis, split_axis=0, concat_axis=0)
+    return jnp.concatenate(blocks, axis=along)
 
 
 def sent_together(arrays, axis, dim, along):
@@ -180,7 +187,7 @@
     tokens = jnp.where(covered[:, None], flat_rows[source_row], jnp.zeros((), jnp.bfloat16))
     packed_ids = jnp.where(covered, flat_ids[source_row], -1).astype(jnp.int32)
     doc_ids = jnp.where(covered, slot_pick, -1)
-    full_rows = lax.all_gather(tokens, "tp", axis=1, tiled=True)
+    full_rows = all_by_exchange(tokens, "tp", 1)
     scaled_input = normalize(full_rows, norm_gain)
     q_width = w_q.shape[1]
     pair_width = key_value_weight.shape[1] * key_value_weight.shape[2]

time: 291 us -> 355 us (1.22)
  local copies, waits for them, and re-layouts: 16.3 us -> 45.9 us
  waiting for transfers between devices: 189 us -> 210 us
  other arithmetic: 18.1 us -> 26.8 us
  starting transfers between devices: 19.1 us -> 25.7 us
    all_to_all x0 -> x1, waiting for transfers between devices: none -> 177 us  [all_by_exchange(): blocks = lax.all_to_all(blocks, mesh_axis, split_axis=0, concat_axis=0)]
    all_gather x1, waiting for transfers between devices: 83.7 us -> 0.01 us  [sent_together(): lax.all_gather(both, axis, axis=dim, tiled=True)]
    all_gather x1 -> x0, waiting for transfers between devices: 75 us -> none  [on_device(): full_rows = lax.all_gather(tokens, 'tp', axis=1, tiled=True)]
    all_to_all x0 -> x1, local copies, waits for them, and re-layouts: none -> 11.4 us  [all_by_exchange(): blocks = lax.all_to_all(blocks, mesh_axis, split_axis=0, concat_axis=0)]
    dot_general x0 -> x2, local copies, waits for them, and re-layouts: none -> 10.8 us  [add_rows(): jnp.dot(columns, piece_rows, preferred_element_type=jnp.float32)]
    all_to_all x0 -> x1, starting transfers between devices: none -> 7.39 us  [all_by_exchange(): blocks = lax.all_to_all(blocks, mesh_axis, split_axis=0, concat_axis=0)]
    another operation x2 -> x3, other arithmetic: 0.9 us -> 5.34 us
    convert_element_type x0 -> x1, other arithmetic: none -> 4.44 us  [normalize(): return (wide * lax.rsqrt(jnp.mean(wide * wide, axis=1, keepdims=True) + e...]
  transfers between devices with their start and end apart: 5 -> 5, of which waited for: 5 -> 3; matrix products, arithmetic and copies ran while one was open for 8% -> 16% of each run, Pallas kernels for 0% -> 0%
where the time goes in v1:
time: 355 us; the launch traced here: 354 us
  waiting for transfers between devices  210 us (59%)
  local copies, waits for them, and re-layouts  45.9 us (13%)
  matrix products  31.7 us (9%)
  other arithmetic  26.8 us (8%)
  starting transfers between devices  25.7 us (7%)
  between operations  14.4 us (4%)
    all_to_all x1, waiting for transfers between devices, all_by_exchange(): blocks = lax.all_to_all(blocks, mesh_axis, split_axis=0, concat_axis=0)  177 us
    all_to_all x1, waiting for transfers between devices, on_device(): lax.all_to_all(slot_rows, 'fsdp', split_axis=0, concat_axis=0, tiled=True)  30.4 us
    dot_general x2, matrix products, add_rows(): jnp.dot(columns, piece_rows, preferred_element_type=jnp.float32)  21.4 us
    all_to_all x1, local copies, waits for them, and re-layouts, all_by_exchange(): blocks = lax.all_to_all(blocks, mesh_axis, split_axis=0, concat_axis=0)  11.4 us
    dot_general x2, local copies, waits for them, and re-layouts, add_rows(): jnp.dot(columns, piece_rows, preferred_element_type=jnp.float32)  10.8 us
    all_to_all x1, starting transfers between devices, on_device(): lax.all_to_all(slot_meta, 'fsdp', split_axis=0, concat_axis=0, tiled=True)  8.58 us
    all_to_all x1, starting transfers between devices, all_by_exchange(): blocks = lax.all_to_all(blocks, mesh_axis, split_axis=0, concat_axis=0)  7.39 us
  transfers between devices with their start and end apart: 5, of which 3 were waited for; matrix products, arithmetic and copies ran while one was open for 16% of the time, Pallas kernels for 0%

profile of v1, /device:TPU:1, one launch (start us, length us, event | category | flops | bytes accessed | tf_op | source)
XLA Modules:
  0.0 354.3 jit_solution(3487129687991338225)
XLA Ops:
  7.2 0.0 copy-start
  7.2 0.0 copy-start.8
  7.2 0.0 all-gather.2.cloned.1.call-start
  7.2 1.1 copy.151
  8.3 1.9 pad_maximum_fusion
  10.3 0.0 all-gather.2.cloned.1.call-update
  10.3 0.9 convert_reduce_fusion
  11.2 0.8 select_reduce_fusion.4
  12.0 0.7 copy.93
  12.7 8.6 %all-to-all-start = ((s32[32,1,2]{2,1,0:T(1,128)}), s32[32,1,2]{2,1,0:T(1,128)S(1)}, u32[]{:S(2)}, u32[]{:S(2)}) async-start(s32[32,1,2]{2,1,0:T(1,128)} %copy.93), calls=%async_computation | async-start | bytes 32768 | tf_op jit(solution)/shard_map/all_to_all | solution.py:168
  21.3 2.2 convert_bitcast_fusion
  23.5 2.5 copy.96
  26.0 2.2 all-to-all-done
  28.2 5.2 %all-to-all-start.2 = ((bf16[32,1,32,1024]{3,2,1,0:T(8,128)(2,1)}), bf16[32,1,32,1024]{3,2,1,0:T(8,128)(2,1)}, u32[]{:S(2)}, u32[]{:S(2)}) async-start(bf16[32,1,32,1024]{3,2,1,0:T(8,128)(2,1)} %copy.96), calls=%async_computation.2 | async-start | bytes 4194304 | tf_op jit(solution)/shard_map/all_to_all | solution.py:166
  33.4 0.1 fusion.56
  33.5 0.7 select_reduce_fusion
  34.2 1.3 slice_reduce_fusion
  35.5 0.1 fusion.53
  35.6 0.1 select_reduce_fusion.1
  35.8 30.4 %all-to-all-done.2 = bf16[32,1,32,1024]{3,2,1,0:T(8,128)(2,1)} async-done(((bf16[32,1,32,1024]{3,2,1,0:T(8,128)(2,1)}), bf16[32,1,32,1024]{3,2,1,0:T(8,128)(2,1)}, u32[]{:S(2)}, u32[]{:S(2)}) %all-to-all-start.2) | async-done | bytes 2097184 | tf_op jit(solution)/shard_map/all_to_all | solution.py:166
  66.2 4.4 %all-to-all-start.1 = ((s32[32,1,32]{2,1,0:T(1,128)}), s32[32,1,32]{2,1,0:T(1,128)S(1)}, u32[]{:S(2)}, u32[]{:S(2)}) async-start(s32[32,1,32]{2,1,0:T(1,128)} %bitcast.18), calls=%async_computation.1 | async-start | bytes 32768 | tf_op jit(solution)/shard_map/all_to_all | solution.py:167
  70.7 5.3 %gather_fusion.1 = bf16[512,1024]{1,0:T(8,128)(2,1)} fusion(bf16[1024,1024]{1,0:T(8,128)(2,1)} %bitcast.24, s32[1024]{0:T(1024)S(1)} %pad_clamp_fusion), kind=kCustom, calls=%fused_computation.1 | custom fusion | bytes 2099200 | tf_op jit(solution)/shard_map/gather | solution.py:187
  76.0 1.7 broadcast_select_fusion
  77.7 0.0 all-to-all-done.1
  77.7 4.4 %stack.11 = bf16[8,512,1024]{2,1,0:T(8,128)(2,1)} broadcast(bf16[512,1024]{1,0:T(8,128)(2,1)S(1)} %broadcast_select_fusion), dimensions={1,2} | broadcast | bytes 9437184 | tf_op jit(solution)/shard_map/stack | solution.py:15
  82.1 0.0 copy-start.5
  82.1 7.4 %all-to-all-start.3 = ((bf16[8,512,1024]{2,1,0:T(8,128)(2,1)}), bf16[8,512,1024]{2,1,0:T(8,128)(2,1)}, u32[]{:S(2)}, u32[]{:S(2)}) async-start(bf16[8,512,1024]{2,1,0:T(8,128)(2,1)} %stack.11), calls=%async_computation.3 | async-start | bytes 16777216 | tf_op jit(solution)/shard_map/all_to_all | solution.py:16
  89.5 0.0 copy-done.7
  89.6 0.1 convolution_multiply_fusion.1
  89.7 0.1 fusion.70
  89.8 0.1 iota_compare_fusion.3
  89.9 0.7 fusion.73
  90.7 0.1 fusion.60
  90.8 0.2 fusion.35
  91.0 0.1 fusion.64
  91.1 0.2 fusion.62
  91.3 2.1 fusion.26
  93.4 0.6 copy.104
  94.0 0.2 fusion.34
  94.2 1.0 multiply_cosine_fusion
  95.2 0.5 broadcast.458
  95.7 0.7 reduce.18
  96.4 0.1 reshape.616
  96.5 2.3 gather_fusion
  98.8 0.6 broadcast_select_fusion.2
  99.4 177.2 %all-to-all-done.3 = bf16[8,512,1024]{2,1,0:T(8,128)(2,1)} async-done(((bf16[8,512,1024]{2,1,0:T(8,128)(2,1)}), bf16[8,512,1024]{2,1,0:T(8,128)(2,1)}, u32[]{:S(2)}, u32[]{:S(2)}) %all-to-all-start.3) | async-done | bytes 8388640 | tf_op jit(solution)/shard_map/all_to_all | solution.py:16
  276.6 11.4 %copy.97 = bf16[8,512,1024]{1,2,0:T(8,128)(2,1)} copy(bf16[8,512,1024]{2,1,0:T(8,128)(2,1)} %all-to-all-done.3) | data formatting | bytes 16777216 | tf_op jit(solution)/shard_map/all_to_all | solution.py:16
  288.0 5.3 %multiply_reduce_fusion = f32[512]{0:T(512)S(1)} fusion(bf16[8,512,1024]{1,2,0:T(8,128)(2,1)} %copy.97), kind=kLoop, calls=%fused_computation.8 | loop fusion | flops 12582400 | bytes 8390656 | tf_op jit(solution)/shard_map/reduce_sum | solution.py:118
  293.3 0.4 copy-done.2
  293.7 4.4 %multiply_convert_fusion = bf16[8,512,1024]{1,2,0:T(8,128)(2,1)} fusion(f32[8,1024]{1,0:T(8,128)S(1)} %mul.182, f32[512]{0:T(512)S(1)} %add_rsqrt_fusion, bf16[8,512,1024]{1,2,0:T(8,128)(2,1)S(1)} %copy-done.2), kind=kLoop, calls=%fused_computation.7 | loop fusion | flops 16777216 | bytes 16812032 | tf_op jit(solution)/shard_map/convert.9
  298.2 4.4 %fusion.3 = bf16[512,8192]{0,1:T(8,128)(2,1)} fusion(f32[8192]{0:T(1024)S(1)} %copy-done.5, f32[512]{0:T(512)S(1)} %add_rsqrt_fusion, bf16[8,512,1024]{1,2,0:T(8,128)(2,1)S(1)} %copy-done.2), kind=kLoop, calls=%fused_computation.6 | loop fusion | flops 16777216 | bytes 16812032 | tf_op jit(solution)/shard_map/convert_element_type | solution.py:120
  302.6 14.4 %add_bitcast_fusion = f32[64,8,8,128]{3,1,2,0:T(8,128)S(1)} fusion(bf16[512,8192]{0,1:T(8,128)(2,1)} %fusion.3, bf16[8192,1280]{1,0:T(8,128)(2,1)} %all-gather.2.cloned.1.call-done, f32[1024]{0:T(1024)S(1)} %copy-done.11), kind=kOutput, calls=%fused_computation.29 | convolution fusion | flops 8590458880 | bytes 27267072 | tf_op jit(solution)/shard_map/dot_general | solution.py:198
  317.0 0.5 copy.124
  317.5 2.7 fusion.72
  320.2 4.4 %slice_bitcast_fusion = bf16[256,8192]{0,1:T(8,128)(2,1)} fusion(bf16[8192,1280]{1,0:T(8,128)(2,1)} %all-gather.2.cloned.1.call-done), kind=kLoop, calls=%fused_computation.18 | loop fusion | bytes 8388608 | tf_op jit(solution)/shard_map/dot_general | solution.py:198
  324.6 6.4 %copy.98 = bf16[256,8192]{1,0:T(8,128)(2,1)} copy(bf16[256,8192]{0,1:T(8,128)(2,1)} %slice_bitcast_fusion) | data formatting | bytes 8388608 | tf_op jit(solution)/shard_map/dot_general | solution.py:198
  331.0 7.0 %convolution_add_fusion = f32[512,2,128]{0,2,1:T(8,128)S(1)} fusion(bf16[512,8192,1]{0,1,2:T(8,128)(2,1)} %bitcast.134, bf16[2,128,8192]{2,1,0:T(8,128)(2,1)} %bitcast.135, f32[2,128]{1,0:T(2,128)S(1)} %copy-done.13), kind=kOutput, calls=%fused_computation.31 | convolution fusion | flops 2147614720 | bytes 13108224 | tf_op jit(solution)/shard_map/dot_general | solution.py:198
  338.0 0.6 fusion.51
  338.6 0.8 subtract_convert_fusion
  339.4 2.2 fusion.5
  341.7 1.7 fusion.4
  343.4 0.0 copy-start.1
  343.4 2.7 fusion.15
  346.2 1.3 copy.105
  (37 shorter events, 0.2 us)
Async XLA Ops:
  7.2 82.7 %copy-start = (bf16[2,4096,128]{2,1,0:T(8,128)(2,1)S(1)}, bf16[2,4096,128]{2,1,0:T(8,128)(2,1)}, u32[]{:S(2)}) copy-start(bf16[2,4096,128]{2,1,0:T(8,128)(2,1)} %param.17) | copy-start | bytes 6291460
  7.2 26.2 %copy-start.8 = (s32[16]{0:T(128)S(1)}, s32[16]{0:T(128)}, u32[]{:S(2)}) copy-start(s32[16]{0:T(128)} %param.25) | copy-start | bytes 196
  7.2 26.3 %copy-start.6 = (s32[16,32]{1,0:T(8,128)S(1)}, s32[16,32]{1,0:T(8,128)}, u32[]{:S(2)}) copy-start(s32[16,32]{1,0:T(8,128)} %param.23) | copy-start | bytes 6148
  7.2 295.4 %all-gather.2.cloned.1.call-start = ((), (), s32[]{:S(2)}) async-start(), calls=%async_computation.4 | async-start | bytes 21626880 | tf_op jit(solution)/shard_map/all_gather | solution.py:26
  12.7 15.5 %all-to-all-start = ((s32[32,1,2]{2,1,0:T(1,128)}), s32[32,1,2]{2,1,0:T(1,128)S(1)}, u32[]{:S(2)}, u32[]{:S(2)}) async-start(s32[32,1,2]{2,1,0:T(1,128)} %copy.93), calls=%async_computation | async-start | bytes 32768 | tf_op jit(solution)/shard_map/all_to_all | solution.py:168
  28.2 38.0 %all-to-all-start.2 = ((bf16[32,1,32,1024]{3,2,1,0:T(8,128)(2,1)}), bf16[32,1,32,1024]{3,2,1,0:T(8,128)(2,1)}, u32[]{:S(2)}, u32[]{:S(2)}) async-start(bf16[32,1,32,1024]{3,2,1,0:T(8,128)(2,1)} %copy.96), calls=%async_computation.2 | async-start | bytes 4194304 | tf_op jit(solution)/shard_map/all_to_all | solution.py:166
  66.2 11.5 %all-to-all-start.1 = ((s32[32,1,32]{2,1,0:T(1,128)}), s32[32,1,32]{2,1,0:T(1,128)S(1)}, u32[]{:S(2)}, u32[]{:S(2)}) async-start(s32[32,1,32]{2,1,0:T(1,128)} %bitcast.18), calls=%async_computation.1 | async-start | bytes 32768 | tf_op jit(solution)/shard_map/all_to_all | solution.py:167
  82.1 7.4 %copy-start.7 = (bf16[2,2,1024]{2,1,0:T(2,128)(2,1)S(1)}, bf16[2,2,1024]{2,1,0:T(2,128)(2,1)}, u32[]{:S(2)}) copy-start(bf16[2,2,1024]{2,1,0:T(2,128)(2,1)} %param.16) | copy-start | bytes 24580
  82.1 7.5 %copy-start.12 = (bf16[2,2,128]{2,1,0:T(2,128)(2,1)S(1)}, bf16[2,2,128]{2,1,0:T(2,128)(2,1)}, u32[]{:S(2)}) copy-start(bf16[2,2,128]{2,1,0:T(2,128)(2,1)} %param.19) | copy-start | bytes 3076
  82.1 7.7 %copy-start.10 = (s32[2]{0:T(128)S(1)}, s32[2]{0:T(128)}, u32[]{:S(2)}) copy-start(s32[2]{0:T(128)} %param.21) | copy-start | bytes 28
  82.1 9.0 %copy-start.9 = (bf16[2,2,128]{2,1,0:T(2,128)(2,1)S(1)}, bf16[2,2,128]{2,1,0:T(2,128)(2,1)}, u32[]{:S(2)}) copy-start(bf16[2,2,128]{2,1,0:T(2,128)(2,1)} %param.20) | copy-start | bytes 3076
  82.1 11.9 %copy-start.5 = (f32[8192]{0:T(1024)S(1)}, f32[8192]{0:T(1024)}, u32[]{:S(2)}) copy-start(f32[8192]{0:T(1024)} %param.27) | copy-start | bytes 98308
  82.1 194.5 %all-to-all-start.3 = ((bf16[8,512,1024]{2,1,0:T(8,128)(2,1)}), bf16[8,512,1024]{2,1,0:T(8,128)(2,1)}, u32[]{:S(2)}, u32[]{:S(2)}) async-start(bf16[8,512,1024]{2,1,0:T(8,128)(2,1)} %stack.11), calls=%async_computation.3 | async-start | bytes 16777216 | tf_op jit(solution)/shard_map/all_to_all | solution.py:16
  288.0 5.8 %copy-start.2 = (bf16[8,512,1024]{1,2,0:T(8,128)(2,1)S(1)}, bf16[8,512,1024]{1,2,0:T(8,128)(2,1)}, u32[]{:S(2)}) copy-start(bf16[8,512,1024]{1,2,0:T(8,128)(2,1)} %copy.97) | copy-start | bytes 25165828
  298.2 4.4 %copy-start.11 = (f32[1024]{0:T(1024)S(1)}, f32[1024]{0:T(1024)}, u32[]{:S(2)}) copy-start(f32[1024]{0:T(1024)} %param.30) | copy-start | bytes 12292
  320.2 10.8 %copy-start.13 = (f32[2,128]{1,0:T(2,128)S(1)}, f32[2,128]{1,0:T(2,128)}, u32[]{:S(2)}) copy-start(f32[2,128]{1,0:T(2,128)} %param.31) | copy-start | bytes 3076
  331.0 7.6 %copy-start.3 = (f32[512,8,64]{2,1,0:T(8,128)S(1)}, f32[512,8,64]{2,1,0:T(8,128)}, u32[]{:S(2)}) copy-start(f32[512,8,64]{2,1,0:T(8,128)} %get-tuple-element.26) | copy-start | bytes 3145732
  331.0 7.6 %copy-start.4 = (f32[512,8,64]{2,1,0:T(8,128)S(1)}, f32[512,8,64]{2,1,0:T(8,128)}, u32[]{:S(2)}) copy-start(f32[512,8,64]{2,1,0:T(8,128)} %get-tuple-element.27) | copy-start | bytes 3145732
  343.4 4.1 %copy-start.1 = (bf16[2,4096,128]{2,1,0:T(8,128)(2,1)S(1)}, bf16[2,4096,128]{2,1,0:T(8,128)(2,1)}, u32[]{:S(2)}) copy-start(bf16[2,4096,128]{2,1,0:T(8,128)(2,1)} %param.17) | copy-start | bytes 6291460
Sparse Core Ops, SparseCore 0:
  10.6 112.9 all-gather.1
